TPU v7x, 32 devices: a whole 2x2x4 slice. The times are simulated.
32 devices in a mesh: inner: 8 (over z, y), cols: 4 (over x, core).
Axes of the slice: x: 2, y: 2, z: 4, core: 2. Of those that a mesh axis runs over, the one named last changes fastest.
Arguments:
- left_u: bfloat16 [64, 512, 128], P(('inner', 'cols')), may hold values from -6 to 6
- left_v: bfloat16 [64, 512, 128], P(('inner', 'cols')), may hold values from -0.0234375 to 0.0234375
- right_u: bfloat16 [16, 64, 512, 128], P('cols', 'inner'), may hold values from -6 to 6
- right_v: bfloat16 [16, 64, 512, 128], P('cols', 'inner'), may hold values from -0.1875 to 0.1875
- sketch: bfloat16 [16, 512, 128], P('cols'), may hold values from -0.25 to 0.25
- tile_index: int32 [16, 64], P('cols', 'inner'), may hold values from 0 to 63, as said below
- slot_mask: int32 [16, 64], P('cols', 'inner'), may hold values from 0 to 1, as said below
Outputs:
- basis: float32 [16, 512, 128], P('cols', 'inner')
- coeff: float32 [16, 512, 128], P('cols', 'inner')
Inputs may be any that keep to these rules, and one draw needn't show every extreme that they name: `tile_index`: slot s of an output tile belongs to inner group g = s // 8 and names a left tile of that group, g * 8 to g * 8 + 7; the tiles named by one output tile's slots of one group are distinct. `slot_mask`: in each output tile and inner group the live slots come first and there is at least one; in every output tile some group has all 8 slots live, and the others at most 4.
All inputs are finite; a program needn't handle non-finite values.
Results may differ from a plain program's by a relative error of at most 0.0045.
Values may be sent and summed in bfloat16 or wider, within the bound.
A program may use at most 64 MiB of HBM per device.

v0:
```python
import math

import jax
import jax.numpy as jnp
from jax import lax
from jax.sharding import PartitionSpec as P

NB = 512


HIGH = lax.Precision.HIGHEST


def orthonormal(sketch_rows, factor):
    solved = jax.scipy.linalg.solve_triangular(factor, jnp.swapaxes(sketch_rows, 1, 2), lower=True)
    return jnp.swapaxes(solved, 1, 2)


def gram_of(sketch_rows):
    return jnp.einsum("ona,onb->oab", sketch_rows, sketch_rows, precision=HIGH)


def body(left_u, left_v, right_u, right_v, sketch, tile_index, slot_mask):
    group_u, group_v = (
        lax.all_gather(left_u, "cols", axis=0, tiled=True),
        lax.all_gather(left_v, "cols", axis=0, tiled=True),
    )
    group_tiles = group_u.shape[0]
    local_idx = tile_index - lax.axis_index("inner") * group_tiles
    live_mask = slot_mask.astype(jnp.float32)[..., None, None]
    tile_u = jnp.take(group_u, local_idx, axis=0)
    tile_v = jnp.take(group_v, local_idx, axis=0)
    pairing = jnp.einsum("osna,osnb->osab", tile_v, right_u, preferred_element_type=jnp.float32)
    probes = jnp.einsum("osnb,ont->osbt", right_v, sketch, preferred_element_type=jnp.float32)
    mixing = (live_mask * jnp.einsum("osab,osbt->osat", pairing, probes, precision=HIGH)).astype(
        jnp.bfloat16
    )
    partial_sketch = jnp.einsum(
        "osna,osat->ont", tile_u, mixing, preferred_element_type=jnp.float32
    )
    scale_up = math.sqrt(NB)
    summed = lax.psum(partial_sketch, "inner")
    factor = jnp.linalg.cholesky(gram_of(summed))
    ortho = orthonormal(summed, factor)
    row_count = summed.shape[1] // lax.axis_size("inner")
    row_start = lax.axis_index("inner") * row_count
    basis = lax.dynamic_slice_in_dim(ortho, row_start, row_count, 1) * scale_up
    full_basis = ortho.astype(jnp.bfloat16)
    projected = jnp.einsum("osna,ont->osat", tile_u, full_basis, preferred_element_type=jnp.float32)
    backward = (
        live_mask * jnp.einsum("osab,osat->osbt", pairing, projected, precision=HIGH)
    ).astype(jnp.bfloat16)
    coeff_terms = jnp.einsum(
        "osnb,osbt->ont", right_v, backward, preferred_element_type=jnp.float32
    )
    coeff = lax.psum_scatter(coeff_terms, "inner", scatter_dimension=1, tiled=True)
    return (basis, coeff)


def solution(mesh):
    return jax.shard_map(
        body,
        mesh=mesh,
        in_specs=(
            P(("inner", "cols"), None, None),
            P(("inner", "cols"), None, None),
            P("cols", "inner", None, None),
            P("cols", "inner", None, None),
            P("cols", None, None),
            P("cols", "inner"),
            P("cols", "inner"),
        ),
        out_specs=(P("cols", "inner", None), P("cols", "inner", None)),
        check_vma=False,
    )
```

profile of v0, /device:TPU:0, one launch (start us, length us, event | category | flops | bytes accessed | tf_op | source)
XLA Modules:
  0.0 335.3 jit_solution(5929237776262730713)
XLA Ops:
  7.2 0.0 copy-start
  7.2 0.0 all-gather.5.cloned.1.call-start
  7.2 0.7 all-gather.5.cloned.1.call-update
  7.9 0.0 all-gather.3.cloned.1.call-start
  8.0 0.7 all-gather.3.cloned.1.call-update
  8.7 0.0 all-reduce.4.cloned.1.call-start
  8.7 0.7 compare_and_fusion
  9.4 0.1 reshape.41
  9.5 0.7 convert_element_type.12
  10.2 0.0 copy-done
  10.2 3.8 %fusion.10 = f32[4,8,128,128]{3,2,1,0:T(8,128)S(1)} fusion(bf16[4,8,512,128]{3,2,1,0:T(8,128)(2,1)} %param.12, bf16[4,512,128]{2,1,0:T(8,128)(2,1)S(1)} %copy-done), kind=kOutput, calls=%fused_computation.16 | convolution fusion | flops 536870912 | bytes 6815744 | tf_op jit(solution)/shard_map/osnb,ont->osbt/dot_general | solution.py:34
  14.0 15.0 %all-gather.5.cloned.1.call-done = bf16[8,512,128]{2,1,0:T(8,128)(2,1)} async-done(((bf16[2,512,128]{2,1,0:T(8,128)(2,1)}), bf16[8,512,128]{2,1,0:T(8,128)(2,1)}) %all-gather.5.cloned.1.call-update) | async-done | bytes 1048592 | tf_op jit(solution)/shard_map/all_gather | solution.py:26
  29.0 4.3 %gather_fusion.1 = bf16[32,512,128]{2,1,0:T(8,128)(2,1)} fusion(bf16[8,512,128]{2,1,0:T(8,128)(2,1)} %all-gather.5.cloned.1.call-done, s32[1024]{0:T(1024)S(1)} %pad_clamp_fusion), kind=kCustom, calls=%fused_computation.1.clone | custom fusion | bytes 8388736 | tf_op jit(solution)/shard_map/jit(_take)/gather | solution.py:32
  33.3 6.3 %copy.23 = bf16[4,8,512,128]{2,3,1,0:T(8,128)(2,1)} copy(bf16[4,8,512,128]{3,2,1,0:T(8,128)(2,1)} %bitcast.43) | data formatting | bytes 8388608 | tf_op jit(solution)/shard_map/jit(_take)/gather | solution.py:32
  39.6 7.7 %all-gather.3.cloned.1.call-done = bf16[8,512,128]{2,1,0:T(8,128)(2,1)} async-done(((bf16[2,512,128]{2,1,0:T(8,128)(2,1)}), bf16[8,512,128]{2,1,0:T(8,128)(2,1)}) %all-gather.3.cloned.1.call-update) | async-done | bytes 1048592 | tf_op jit(solution)/shard_map/all_gather | solution.py:25
  47.3 4.3 %gather_fusion = bf16[32,512,128]{2,1,0:T(8,128)(2,1)} fusion(bf16[8,512,128]{2,1,0:T(8,128)(2,1)} %all-gather.3.cloned.1.call-done, s32[1024]{0:T(1024)S(1)} %pad_clamp_fusion), kind=kCustom, calls=%fused_computation.clone | custom fusion | bytes 8388736 | tf_op jit(solution)/shard_map/jit(_take)/gather | solution.py:31
  51.6 6.2 %copy.22 = bf16[4,8,512,128]{2,3,1,0:T(8,128)(2,1)} copy(bf16[4,8,512,128]{3,2,1,0:T(8,128)(2,1)} %bitcast.42) | data formatting | bytes 8388608 | tf_op jit(solution)/shard_map/jit(_take)/gather | solution.py:31
  57.7 4.8 %fusion = f32[4,8,128,128]{3,2,1,0:T(8,128)S(1)} fusion(bf16[4,8,512,128]{3,2,1,0:T(8,128)(2,1)} %param.11, bf16[4,8,512,128]{2,3,1,0:T(8,128)(2,1)} %copy.23, pred[4,8]{1,0:T(4,128)(4,1)S(1)} %get-tuple-element.9), kind=kOutput, calls=%fused_computation.2 | convolution fusion | flops 538968064 | bytes 10485792 | tf_op jit(solution)/shard_map/osna,osnb->osab/dot_general | solution.py:33
  62.5 0.0 copy-start.3
  62.6 1.3 copy-done.3
  63.9 0.0 copy-start.5
  63.9 2.3 multiply_convert_fusion.1
  66.2 0.0 copy-done.5
  66.2 2.8 fusion.8
  69.0 0.0 all-reduce.4.cloned.1.call-update
  69.0 0.2 all-reduce.6.cloned.1.call-start
  69.3 78.1 %all-reduce.4.cloned.1.call-done = f32[4,512,128]{2,1,0:T(8,128)} async-done(((f32[4,512,128]{2,1,0:T(8,128)}), f32[4,512,128]{2,1,0:T(8,128)}) %all-reduce.4.cloned.1.call-update) | async-done | bytes 1048592 | tf_op jit(solution)/shard_map/psum | solution.py:42
  147.4 0.0 copy-start.2
  147.4 3.4 %fusion.19 = f32[4,128,128]{2,1,0:T(8,128)S(1)} fusion(f32[4,512,128]{2,1,0:T(8,128)} %all-reduce.4.cloned.1.call-done), kind=kOutput, calls=%fused_computation.36 | convolution fusion | flops 402653184 | bytes 1310720 | tf_op jit(solution)/shard_map/ona,onb->oab/dot_general | solution.py:20
  150.8 0.1 copy.27
  151.0 46.9 %custom-call.8 = f32[4,128,128]{2,1,0:T(8,128)S(1)} custom-call(f32[4,128,128]{2,1,0:T(8,128)S(1)} %fusion.15), custom_call_target="Cholesky" | custom-call | tf_op jit(solution)/shard_map/jit(cholesky)/cholesky | solution.py:43
  198.0 0.1 compare_reduce_fusion
  198.1 0.1 select_bitcast_fusion
  198.2 39.5 %custom-call.9 = f32[4,1,128,128]{2,3,1,0:T(8,128)S(1)} custom-call(f32[4,1,128,128]{3,2,1,0:T(8,128)S(1)} %select_bitcast_fusion), custom_call_target="InvertDiagBlocksLowerTriangular" | custom-call | tf_op jit(solution)/shard_map/jit(_solve_triangular)/vmap()/triangular_solve | solution.py:15
  237.7 0.0 copy-done.2
  237.7 1.0 fusion.13
  238.8 0.0 copy-start.4
  238.8 3.6 %fusion.3 = f32[4,8,128,128]{3,2,1,0:T(8,128)S(1)} fusion(bf16[4,8,512,128]{2,3,1,0:T(8,128)(2,1)} %copy.22, pred[4,8]{1,0:T(4,128)(4,1)S(1)} %get-tuple-element.9, f32[4,512,128]{2,1,0:T(8,128)S(1)} %fusion.13), kind=kOutput, calls=%fused_computation.6 | convolution fusion | flops 539230208 | bytes 7340064 | tf_op jit(solution)/shard_map/osna,ont->osat/dot_general | solution.py:49
  242.4 0.0 copy-done.4
  242.4 0.0 copy-start.1
  242.5 3.7 %multiply_convert_fusion = bf16[4,8,128,128]{3,2,1,0:T(8,128)(2,1)S(1)} fusion(f32[4,8,128,128]{3,2,1,0:T(8,128)S(1)} %copy-done.4, f32[4,8,128,128]{3,2,1,0:T(8,128)S(1)} %fusion.3, f32[4,8]{1,0:T(4,128)S(1)} %convert_element_type.12), kind=kOutput, calls=%fused_computation.11 | convolution fusion | flops 806354944 | bytes 5243008 | tf_op jit(solution)/shard_map/osab,osat->osbt/dot_general | solution.py:51
  246.2 0.0 copy-done.1
  246.2 0.0 copy-start.6
  246.2 1.5 convolution_bitcast_fusion
  247.7 1.4 copy.31
  249.1 0.0 all-reduce.6.cloned.1.call-update
  249.1 0.0 copy-done.6
  249.2 0.6 dynamic-slice
  250.4 0.7 dynamic-slice_multiply_fusion
  251.1 76.1 %all-reduce.6.cloned.1.call-done = f32[4,512,128]{2,0,1:T(4,128)} async-done(((f32[4,512,128]{2,0,1:T(4,128)}), f32[4,512,128]{2,0,1:T(4,128)}) %all-reduce.6.cloned.1.call-update) | async-done | bytes 1048592
  327.2 0.9 constant_dynamic-slice_fusion
  328.1 0.7 copy.32
  (5 shorter events, 0.1 us)
Async XLA Ops:
  7.2 3.0 copy-start
  7.2 21.8 %all-gather.5.cloned.1.call-start = ((), (), s32[]{:S(2)}) async-start(), calls=%async_computation.1 | async-start | bytes 1310720 | tf_op jit(solution)/shard_map/all_gather | solution.py:26
  7.9 39.4 %all-gather.3.cloned.1.call-start = ((), (), s32[]{:S(2)}) async-start(), calls=%async_computation | async-start | bytes 1310720 | tf_op jit(solution)/shard_map/all_gather | solution.py:25
  8.7 138.7 %all-reduce.4.cloned.1.call-start = ((), (), s32[]{:S(2)}) async-start(), calls=%async_computation.2 | async-start | bytes 2097152 | tf_op jit(solution)/shard_map/psum | solution.py:42
  62.5 1.3 copy-start.3
  63.9 2.3 copy-start.5
  69.0 258.2 %all-reduce.6.cloned.1.call-start = ((), (), s32[]{:S(2)}) async-start(), calls=%async_computation.3 | async-start | bytes 2097152
  147.4 90.3 %copy-start.2 = (f32[4,512,128]{2,1,0:T(8,128)S(1)}, f32[4,512,128]{2,1,0:T(8,128)}, u32[]{:S(2)}) copy-start(f32[4,512,128]{2,1,0:T(8,128)} %all-reduce.4.cloned.1.call-done) | copy-start | bytes 3145732
  238.8 3.7 %copy-start.4 = (f32[4,8,128,128]{3,2,1,0:T(8,128)S(1)}, f32[4,8,128,128]{3,2,1,0:T(8,128)}, u32[]{:S(2)}) copy-start(f32[4,8,128,128]{3,2,1,0:T(8,128)} %copy-done.3) | copy-start | bytes 6291460
  242.4 3.8 %copy-start.1 = (bf16[4,8,512,128]{3,2,1,0:T(8,128)(2,1)S(1)}, bf16[4,8,512,128]{3,2,1,0:T(8,128)(2,1)}, u32[]{:S(2)}) copy-start(bf16[4,8,512,128]{3,2,1,0:T(8,128)(2,1)} %param.12) | copy-start | bytes 12582916
  246.2 2.9 copy-start.6
Sparse Core Ops, SparseCore 0:
  9.5 19.4 all-gather.4
  30.6 16.6 all-gather.2
  69.1 78.2 all-reduce.3
  249.3 77.8 all-reduce.5
where the time goes:
time: 336 us; the launch traced here: 335 us
  waiting for transfers between devices  178 us (53%)
  other arithmetic  88.8 us (26%)
  matrix products  27 us (8%)
  local copies, waits for them, and re-layouts  26.1 us (8%)
  between operations  14.6 us (4%)
    psum x1, waiting for transfers between devices, body(): summed = lax.psum(partial_sketch, 'inner')  78.1 us
    unnamed x5, waiting for transfers between devices  77.5 us
    another operation x4, other arithmetic, body(): factor = jnp.linalg.cholesky(gram_of(summed))  47.1 us
    another operation x3, other arithmetic, orthonormal(): jax.scipy.linalg.solve_triangular(factor, jnp.swapaxes(sketch_rows, 1, 2)...  39.7 us
    all_gather x1, waiting for transfers between devices, body(): lax.all_gather(left_v, 'cols', axis=0, tiled=True)  15 us
    gather x2, local copies, waits for them, and re-layouts, body(): tile_v = jnp.take(group_v, local_idx, axis=0)  10.6 us
    gather x2, local copies, waits for them, and re-layouts, body(): tile_u = jnp.take(group_u, local_idx, axis=0)  10.5 us
    all_gather x1, waiting for transfers between devices, body(): lax.all_gather(left_u, 'cols', axis=0, tiled=True)  7.72 us
  transfers between devices with their start and end apart: 4, of which 4 were waited for; matrix products, arithmetic and copies ran while one was open for 5% of the time, Pallas kernels for 0%

commit v1 on v0

v1 whole, which is shorter than its diff:
```python
import functools
import math

import jax
import jax.numpy as jnp
from jax import lax
from jax.experimental import pallas as pl
from jax.experimental.pallas import tpu as pltpu
from jax.sharding import PartitionSpec as P

MESH = pl.DeviceIdType.MESH
F32 = jnp.float32
BF16 = jnp.bfloat16
NN = (((1,), (0,)), ((), ()))
NT = (((1,), (1,)), ((), ()))
TN = (((0,), (0,)), ((), ()))


def mm(a, b, dims):
    return lax.dot_general(a, b, dims, preferred_element_type=F32)


def split(a):
    hi = a.astype(BF16)
    return hi, (a - hi.astype(F32)).astype(BF16)


def mm_f32(a, b, dims):
    return lax.dot_general(a, b, dims, precision=lax.Precision.HIGHEST, preferred_element_type=F32)


def kernel(
    n_in, n_co, left_u, left_v, right_u, right_v, sketch, index, mask, basis, coeff,
    ug, vg, vt, ru, rv, sk, phi, plo, mix, ybuf, sbuf, r1, s2f, s2b, r2, yrow, yb,
    cbuf, csbuf, cr1, cs2f, cs2b, cr2, crow, xm, scale,
    load_sem, gs_sem, gr_sem, rs_send, rs_recv, ag_send, ag_recv,
):
    nx = n_co // 2
    ny = nx
    nz = n_in // ny
    tpd = left_u.shape[0]
    tiles = tpd * n_co
    n_out, slots, nb, rk = right_u.shape
    rows = nb // n_in
    me_in = lax.axis_index("inner")
    me_co = lax.axis_index("cols")
    x, core = lax.div(me_co, 2), lax.rem(me_co, 2)
    z, y = lax.div(me_in, ny), lax.rem(me_in, ny)

    def co_at(dx):
        return lax.rem(x + dx, nx) * 2 + core

    partner = x * 2 + (1 - core)

    def z_at(dz):
        return lax.rem(z + dz, nz) * ny + y

    def y_at(dy):
        return z * ny + lax.rem(y + dy, ny)

    sends = []

    def remote(src, dst, s_sem, r_sem, **dev):
        return pltpu.make_async_remote_copy(
            src_ref=src, dst_ref=dst, send_sem=s_sem, recv_sem=r_sem,
            device_id=dev, device_id_type=MESH,
        )

    def go(copy):
        copy.start()
        sends.append(copy)

    loads = []
    for j in range(n_out):
        for num, (src, dst) in enumerate(((sketch, sk), (right_v, rv), (right_u, ru))):
            loads.append(pltpu.make_async_copy(src.at[j], dst.at[j], load_sem.at[j, num]))
    own = pl.ds(me_co * tpd, tpd)
    own_v = pltpu.make_async_copy(left_v, vg.at[own], load_sem.at[n_out, 0])
    own_u = pltpu.make_async_copy(left_u, ug.at[own], load_sem.at[n_out, 1])
    for c in [own_v, own_u] + loads:
        c.start()

    barrier = pltpu.get_barrier_semaphore()
    for dx in range(1, nx):
        pl.semaphore_signal(barrier, inc=1, device_id={"cols": co_at(dx)}, device_id_type=MESH)
    pl.semaphore_signal(barrier, inc=1, device_id={"cols": partner}, device_id_type=MESH)
    for dy in range(1, ny):
        pl.semaphore_signal(barrier, inc=1, device_id={"inner": y_at(dy)}, device_id_type=MESH)
    for dz in range(1, nz):
        pl.semaphore_signal(barrier, inc=1, device_id={"inner": z_at(dz)}, device_id_type=MESH)
    pl.semaphore_wait(barrier, nx - 1 + 1 + ny - 1 + nz - 1)

    for num, (src, dst) in enumerate(((left_v, vg), (left_u, ug))):
        for dx in range(1, nx):
            go(remote(src, dst.at[own], gs_sem.at[num, dx], gr_sem.at[num, dx], cols=co_at(dx)))
        go(remote(src, dst.at[own], gs_sem.at[num, 0], gr_sem.at[num, 0], cols=partner))

    def block(dst, position):
        return dst.at[pl.ds(position * tpd, tpd)]

    def forward(num, dst):
        for dx in range(1, nx):
            part = block(dst, co_at(nx - dx))
            remote(part, part, gs_sem.at[num, dx], gr_sem.at[num, dx], cols=partner).wait_recv()
            go(remote(part, part, gs_sem.at[num, nx + dx], gr_sem.at[num, nx + dx], cols=partner))

    def gathered(num, dst):
        part = block(dst, partner)
        remote(part, part, gs_sem.at[num, 0], gr_sem.at[num, 0], cols=partner).wait_recv()
        for dx in range(1, nx):
            part = block(dst, lax.rem(x + nx - dx, nx) * 2 + (1 - core))
            remote(part, part, gs_sem.at[num, nx + dx], gr_sem.at[num, nx + dx], cols=partner).wait_recv()

    for c in loads:
        c.wait()
    forward(0, vg)
    gathered(0, vg)
    own_v.wait()
    own_u.wait()

    @pl.loop(0, tiles)
    def _(t):
        vt[t] = jnp.transpose(vg[t])

    for j in range(n_out):
        om = jnp.transpose(sk[j])

        @pl.loop(0, slots)
        def _(s, j=j, om=om):
            k = lax.rem(index[j, s], tiles)
            live = mask[j, s].astype(F32)
            probe_hi, probe_lo = split(mm(om, rv[j, s], NN))
            pair_hi, pair_lo = split(mm(vt[k], ru[j, s], NN))
            phi[j, s] = pair_hi
            plo[j, s] = pair_lo
            mixed = mm(pair_hi, probe_hi, NT) + mm(pair_hi, probe_lo, NT) + mm(pair_lo, probe_hi, NT)
            mix[j, s] = (mixed * live).astype(BF16)

        if j == 0:
            forward(1, ug)

    gathered(1, ug)

    def scatter_first(phase, j, total, buf, sb, first):
        buf[j] = total.reshape(nz, ny, rows, rk)
        low = total.astype(BF16).reshape(nz, ny, rows, rk)
        for yy in range(ny):
            sb[j, yy] = low[:, yy]
        for dy in range(1, ny):
            go(remote(
                sb.at[j, lax.rem(y + dy, ny)], first.at[j, dy],
                rs_send.at[phase, j, dy], rs_recv.at[phase, j, dy], inner=y_at(dy),
            ))

    def scatter_second(phase, j, buf, sb, first, sumf, sumb, second):
        total = buf[j, :, y]
        for dy in range(1, ny):
            part = first.at[j, dy]
            remote(part, part, rs_send.at[phase, j, dy], rs_recv.at[phase, j, dy], inner=y_at(dy)).wait_recv()
            total = total + first[j, dy].astype(F32)
        sumf[j] = total
        sumb[j] = total.astype(BF16)
        for dz in range(1, nz):
            go(remote(
                sumb.at[j, lax.rem(z + dz, nz)], second.at[j, dz],
                rs_send.at[phase, j, ny + dz], rs_recv.at[phase, j, ny + dz], inner=z_at(dz),
            ))

    def scatter_last(phase, j, sumf, second):
        total = sumf[j, z]
        for dz in range(1, nz):
            part = second.at[j, dz]
            remote(part, part, rs_send.at[phase, j, ny + dz], rs_recv.at[phase, j, ny + dz], inner=z_at(dz)).wait_recv()
            total = total + second[j, dz].astype(F32)
        return total

    for j in range(n_out):
        total = mm(ug[lax.rem(index[j, 0], tiles)], mix[j, 0], NN)
        for s in range(1, slots):
            total = total + mm(ug[lax.rem(index[j, s], tiles)], mix[j, s], NN)
        scatter_first(0, j, total, ybuf, sbuf, r1)
    for j in range(n_out):
        scatter_second(0, j, ybuf, sbuf, r1, s2f, s2b, r2)

    for j in range(n_out):
        total = scatter_last(0, j, s2f, r2)
        yrow[j] = total
        yb[j, me_in] = total.astype(BF16)
        part = yb.at[j, me_in]
        for dz in range(1, nz):
            go(remote(part, part, ag_send.at[j, 0, dz], ag_recv.at[j, 0, dz], inner=z_at(dz)))
        for dy in range(1, ny):
            go(remote(part, part, ag_send.at[j, dy, 0], ag_recv.at[j, dy, 0], inner=y_at(dy)))
    for j in range(n_out):
        for dz in range(1, nz):
            part = yb.at[j, z_at(nz - dz)]
            remote(part, part, ag_send.at[j, 0, dz], ag_recv.at[j, 0, dz], inner=z_at(dz)).wait_recv()
            for dy in range(1, ny):
                go(remote(part, part, ag_send.at[j, dy, dz], ag_recv.at[j, dy, dz], inner=y_at(dy)))

    for j in range(n_out):
        for dy in range(1, ny):
            for dz in range(nz):
                pos = lax.rem(z + nz - dz, nz) * ny + lax.rem(y + ny - dy, ny)
                part = yb.at[j, pos]
                remote(part, part, ag_send.at[j, dy, dz], ag_recv.at[j, dy, dz], inner=y_at(dy)).wait_recv()
        summed_t = jnp.transpose(yb[j].reshape(nb, rk))

        def step(s, total, j=j, summed_t=summed_t):
            live = mask[j, s].astype(F32)
            z_hi, z_lo = split(mm(summed_t, ug[lax.rem(index[j, s], tiles)], NN))
            back = mm(z_hi, phi[j, s], NN) + mm(z_hi, plo[j, s], NN) + mm(z_lo, phi[j, s], NN)
            b_hi, b_lo = split(back * live)
            return total + (mm(rv[j, s], b_hi, NT) + mm(rv[j, s], b_lo, NT))

        total = lax.fori_loop(0, slots, step, jnp.zeros((nb, rk), F32))
        scatter_first(1, j, total, cbuf, csbuf, cr1)

    row_id = lax.broadcasted_iota(jnp.int32, (rk, rk), 0)
    col_id = lax.broadcasted_iota(jnp.int32, (rk, rk), 1)
    lane = lax.broadcasted_iota(jnp.int32, (1, rk), 1)
    for j in range(n_out):
        summed = yb[j].reshape(nb, rk)
        gram = mm(summed, summed, TN)
        diag = jnp.where(row_id == col_id, gram, 0.0)
        s_row = lax.rsqrt(jnp.sum(diag, axis=0, keepdims=True))
        s_col = lax.rsqrt(jnp.sum(diag, axis=1, keepdims=True))
        scale[j] = s_row
        xm[j] = gram * s_col * s_row

    def eliminate(start, stop):
        ids = lax.broadcasted_iota(jnp.int32, (rk - start, 1), 0) + start
        at = pl.ds(start, rk - start)

        @pl.loop(start, stop)
        def _(k):
            hot = lane == k
            for j in range(n_out):
                block_x = xm[j, at]
                row = xm[j, pl.ds(k, 1)]
                pivot = jnp.sum(jnp.where(hot, row, 0.0), axis=1, keepdims=True)
                col = jnp.sum(jnp.where(hot, block_x, 0.0), axis=1, keepdims=True)
                weight = jnp.where(ids > k, col * (1.0 / pivot), 0.0)
                xm[j, at] = block_x - weight * (row + jnp.where(hot, 1.0, 0.0))

    piece = rk // 8
    for b in range(3):
        eliminate(b * piece, (b + 1) * piece)
    for j in range(n_out):
        scatter_second(1, j, cbuf, csbuf, cr1, cs2f, cs2b, cr2)
    for b in range(3, 8):
        eliminate(b * piece, (b + 1) * piece)

    for j in range(n_out):
        work = xm[j]
        pivots = jnp.sum(jnp.where(row_id == col_id, work, 0.0), axis=1, keepdims=True)
        lower = jnp.where(col_id < row_id, work, jnp.where(row_id == col_id, 1.0, 0.0))
        inverse = lower * lax.rsqrt(pivots) * scale[j]
        basis[j] = mm_f32(yrow[j], inverse, NT) * math.sqrt(nb)
        coeff[j] = mm_f32(scatter_last(1, j, cs2f, cr2), inverse, NT)

    for copy in sends:
        copy.wait_send()


def body(n_in, n_co, left_u, left_v, right_u, right_v, sketch, tile_index, slot_mask):
    n_out, slots, nb, rk = right_u.shape
    tiles = left_u.shape[0] * n_co
    nx = n_co // 2
    ny = nx
    nz = n_in // ny
    rows = nb // n_in
    wire = [
        pltpu.VMEM((n_out, nz, ny, rows, rk), F32),
        pltpu.VMEM((n_out, ny, nz, rows, rk), BF16),
        pltpu.VMEM((n_out, ny, nz, rows, rk), BF16),
        pltpu.VMEM((n_out, nz, rows, rk), F32),
        pltpu.VMEM((n_out, nz, rows, rk), BF16),
        pltpu.VMEM((n_out, nz, rows, rk), BF16),
        pltpu.VMEM((n_out, rows, rk), F32),
    ]
    out = jax.ShapeDtypeStruct((n_out, rows, rk), F32)
    hbm = pl.BlockSpec(memory_space=pl.ANY)
    smem = pl.BlockSpec(memory_space=pltpu.SMEM)
    vmem = pl.BlockSpec(memory_space=pltpu.VMEM)
    return pl.pallas_call(
        functools.partial(kernel, n_in, n_co),
        out_shape=(out, out),
        in_specs=[hbm] * 5 + [smem] * 2,
        out_specs=(vmem, vmem),
        scratch_shapes=[
            pltpu.VMEM((tiles, nb, rk), BF16),
            pltpu.VMEM((tiles, nb, rk), BF16),
            pltpu.VMEM((tiles, rk, nb), BF16),
            pltpu.VMEM((n_out, slots, nb, rk), BF16),
            pltpu.VMEM((n_out, slots, nb, rk), BF16),
            pltpu.VMEM((n_out, nb, rk), BF16),
            pltpu.VMEM((n_out, slots, rk, rk), BF16),
            pltpu.VMEM((n_out, slots, rk, rk), BF16),
            pltpu.VMEM((n_out, slots, rk, rk), BF16),
        ]
        + wire
        + [pltpu.VMEM((n_out, n_in, rows, rk), BF16)]
        + wire
        + [
            pltpu.VMEM((n_out, rk, rk), F32),
            pltpu.VMEM((n_out, 1, rk), F32),
            pltpu.SemaphoreType.DMA((n_out + 1, 3)),
            pltpu.SemaphoreType.DMA((2, 2 * nx)),
            pltpu.SemaphoreType.DMA((2, 2 * nx)),
            pltpu.SemaphoreType.DMA((2, n_out, ny + nz)),
            pltpu.SemaphoreType.DMA((2, n_out, ny + nz)),
            pltpu.SemaphoreType.DMA((n_out, ny, nz)),
            pltpu.SemaphoreType.DMA((n_out, ny, nz)),
        ],
        compiler_params=pltpu.CompilerParams(
            collective_id=0, has_side_effects=True, vmem_limit_bytes=60 * 1024 * 1024
        ),
    )(left_u, left_v, right_u, right_v, sketch, tile_index, slot_mask)


def solution(mesh):
    return jax.shard_map(
        functools.partial(body, mesh.shape["inner"], mesh.shape["cols"]),
        mesh=mesh,
        in_specs=(
            P(("inner", "cols"), None, None),
            P(("inner", "cols"), None, None),
            P("cols", "inner", None, None),
            P("cols", "inner", None, None),
            P("cols", None, None),
            P("cols", "inner"),
            P("cols", "inner"),
        ),
        out_specs=(P("cols", "inner", None), P("cols", "inner", None)),
        check_vma=False,
    )
```

time: 336 us -> 123 us (0.37)
  waiting for transfers between devices: 178 us -> 0 us
  Pallas kernels: 0 us -> 119 us
  other arithmetic: 88.8 us -> 0 us
  matrix products: 27 us -> 0 us
  local copies, waits for them, and re-layouts: 26.1 us -> 3.14 us
  between operations: 14.6 us -> 0.64 us
    pallas_call x0 -> x1, Pallas kernels: none -> 119 us  [body(): pl.pallas_call(functools.partial(kernel, n_in, n_co), out_shape=(out, out...]
    another operation x7 -> x0, other arithmetic: 86.7 us -> none  [the longest x4 47.1 us: body(): factor = jnp.linalg.cholesky(gram_of(summed))]
    psum x1 -> x0, waiting for transfers between devices: 78.1 us -> none  [body(): summed = lax.psum(partial_sketch, 'inner')]
    unnamed x5 -> x0, waiting for transfers between devices: 77.5 us -> none
    dot_general x8 -> x0, matrix products: 26 us -> none  [the longest x1 4.79 us: body(): jnp.einsum('osna,osnb->osab', tile_v, right_u, preferred_element_type=jnp...]
    all_gather x2 -> x0, waiting for transfers between devices: 22.7 us -> none  [the longest x1 15 us: body(): lax.all_gather(left_v, 'cols', axis=0, tiled=True)]
    gather x4 -> x0, local copies, waits for them, and re-layouts: 21 us -> none  [the longest x2 10.6 us: body(): tile_v = jnp.take(group_v, local_idx, axis=0)]
  transfers between devices with their start and end apart: 4 -> 0, of which waited for: 4 -> 0; matrix products, arithmetic and copies ran while one was open for 5% -> 0% of each run, Pallas kernels for 0% -> 0%
where the time goes in v1:
time: 123 us
  Pallas kernels  119 us (97%)
  local copies, waits for them, and re-layouts  3.14 us (3%)
    pallas_call x1, Pallas kernels, body(): pl.pallas_call(functools.partial(kernel, n_in, n_co), out_shape=(out, out...  119 us
    unnamed x2, local copies, waits for them, and re-layouts  3.14 us

profile of v1, /device:TPU:0, one launch (start us, length us, event | category | flops | bytes accessed | tf_op | source)
XLA Modules:
  0.0 122.9 jit_solution(5441286886436552303)
XLA Ops:
  0.6 119.1 %shard_map.86 = (f32[4,64,128]{2,1,0:T(8,128)}, f32[4,64,128]{2,1,0:T(8,128)}) custom-call(bf16[2,512,128]{2,1,0:T(8,128)(2,1)} %left_u.1, bf16[2,512,128]{2,1,0:T(8,128)(2,1)} %left_v.1, bf16[4,8,512,128]{3,2,1,0:T(8,128)(2,1)} %right_u.1, bf16[4,8,512,128]{3,2,1,0:T(8,128)(2,1)} %right_v.1, bf16[4,512,128]{2,1,0:T(8,128)(2,1)} %sketch.1, s32[4,8]{1,0:T(4,128)} %index.1, ...), custom_call_target="tpu_custom_call" | custom-call | tf_op jit(solution)/shard_map/pallas_call | solution.py:286
  119.8 1.6 %copy.11 = f32[4,64,128]{2,1,0:T(8,128)} copy(f32[4,64,128]{2,1,0:T(8,128)} %get-tuple-element.4) | data formatting | bytes 262144
  121.3 1.6 %copy.12 = f32[4,64,128]{2,1,0:T(8,128)} copy(f32[4,64,128]{2,1,0:T(8,128)} %get-tuple-element.5) | data formatting | bytes 262144

commit v2 on v1

--- a/solution.py
+++ b/solution.py
@@ -32,7 +32,7 @@
 def kernel(
     n_in, n_co, left_u, left_v, right_u, right_v, sketch, index, mask, basis, coeff,
     ug, vg, vt, ru, rv, sk, phi, plo, mix, ybuf, sbuf, r1, s2f, s2b, r2, yrow, yb,
-    cbuf, csbuf, cr1, cs2f, cs2b, cr2, crow, xm, scale,
+    cbuf, csbuf, cr1, cs2f, cs2b, cr2, crow, xm, scale, bt,
     load_sem, gs_sem, gr_sem, rs_send, rs_recv, ag_send, ag_recv,
 ):
     nx = n_co // 2
@@ -125,16 +125,16 @@
     for j in range(n_out):
         om = jnp.transpose(sk[j])
 
-        @pl.loop(0, slots)
-        def _(s, j=j, om=om):
-            k = lax.rem(index[j, s], tiles)
-            live = mask[j, s].astype(F32)
-            probe_hi, probe_lo = split(mm(om, rv[j, s], NN))
-            pair_hi, pair_lo = split(mm(vt[k], ru[j, s], NN))
-            phi[j, s] = pair_hi
-            plo[j, s] = pair_lo
-            mixed = mm(pair_hi, probe_hi, NT) + mm(pair_hi, probe_lo, NT) + mm(pair_lo, probe_hi, NT)
-            mix[j, s] = (mixed * live).astype(BF16)
+        @pl.loop(0, slots // 4)
+        def _(quad, j=j, om=om):
+            for s in [quad * 4 + i for i in range(4)]:
+                live = mask[j, s].astype(F32)
+                probe_hi, probe_lo = split(mm(om, rv[j, s], NN))
+                pair_hi, pair_lo = split(mm(vt[lax.rem(index[j, s], tiles)], ru[j, s], NN))
+                phi[j, s] = pair_hi
+                plo[j, s] = pair_lo
+                mixed = mm(pair_hi, probe_hi, NT) + mm(pair_hi, probe_lo, NT) + mm(pair_lo, probe_hi, NT)
+                mix[j, s] = (mixed * live).astype(BF16)
 
         if j == 0:
             forward(1, ug)
@@ -206,19 +206,24 @@
                 remote(part, part, ag_send.at[j, dy, dz], ag_recv.at[j, dy, dz], inner=y_at(dy)).wait_recv()
         summed_t = jnp.transpose(yb[j].reshape(nb, rk))
 
-        def step(s, total, j=j, summed_t=summed_t):
-            live = mask[j, s].astype(F32)
-            z_hi, z_lo = split(mm(summed_t, ug[lax.rem(index[j, s], tiles)], NN))
-            back = mm(z_hi, phi[j, s], NN) + mm(z_hi, plo[j, s], NN) + mm(z_lo, phi[j, s], NN)
-            b_hi, b_lo = split(back * live)
-            return total + (mm(rv[j, s], b_hi, NT) + mm(rv[j, s], b_lo, NT))
-
-        total = lax.fori_loop(0, slots, step, jnp.zeros((nb, rk), F32))
+        @pl.loop(0, slots // 4)
+        def _(quad, j=j, summed_t=summed_t):
+            for s in [quad * 4 + i for i in range(4)]:
+                live = mask[j, s].astype(F32)
+                z_hi, z_lo = split(mm(summed_t, ug[lax.rem(index[j, s], tiles)], NN))
+                back = mm(z_hi, phi[j, s], NN) + mm(z_hi, plo[j, s], NN) + mm(z_lo, phi[j, s], NN)
+                b_hi, b_lo = split(back * live)
+                bt[j, s, :rk] = b_hi
+                bt[j, s, rk:] = b_lo
+
+        wide = mm(rv[j, 0], bt[j, 0], NT)
+        for s in range(1, slots):
+            wide = wide + mm(rv[j, s], bt[j, s], NT)
+        total = wide[:, :rk] + wide[:, rk:]
         scatter_first(1, j, total, cbuf, csbuf, cr1)
 
     row_id = lax.broadcasted_iota(jnp.int32, (rk, rk), 0)
     col_id = lax.broadcasted_iota(jnp.int32, (rk, rk), 1)
-    lane = lax.broadcasted_iota(jnp.int32, (1, rk), 1)
     for j in range(n_out):
         summed = yb[j].reshape(nb, rk)
         gram = mm(summed, summed, TN)
@@ -228,28 +233,46 @@
         scale[j] = s_row
         xm[j] = gram * s_col * s_row
 
+    sub8 = lax.broadcasted_iota(jnp.int32, (8, rk), 0)
+    lane8 = lax.broadcasted_iota(jnp.int32, (8, rk), 1)
+
     def eliminate(start, stop):
-        ids = lax.broadcasted_iota(jnp.int32, (rk - start, 1), 0) + start
-        at = pl.ds(start, rk - start)
-
         @pl.loop(start, stop)
-        def _(k):
-            hot = lane == k
+        def _(b):
+            base = pl.multiple_of(b * 8, 8)
+            near = lane8 - base
+            at = pl.ds(base, 8)
+            slabs = [xm[j, at] for j in range(n_out)]
+            cols = [
+                [
+                    jnp.broadcast_to(jnp.sum(jnp.where(near == i, slab, 0.0), axis=1, keepdims=True), (8, rk))
+                    for i in range(8)
+                ]
+                for slab in slabs
+            ]
+            pivots = [jnp.ones((8, rk), F32)] * n_out
+            for k in range(8):
+                hot = jnp.where(near[:1] == k, 1.0, 0.0)
+                for j in range(n_out):
+                    column = cols[j][k]
+                    pivots[j] = jnp.where(sub8 == k, column[k : k + 1], pivots[j])
+                    weight = jnp.where(sub8 > k, column * (1.0 / column[k : k + 1]), 0.0)
+                    slabs[j] = slabs[j] - weight * (slabs[j][k : k + 1] + hot)
+                    for i in range(k + 1, 8):
+                        cols[j][i] = cols[j][i] - weight * cols[j][i][k : k + 1]
             for j in range(n_out):
-                block_x = xm[j, at]
-                row = xm[j, pl.ds(k, 1)]
-                pivot = jnp.sum(jnp.where(hot, row, 0.0), axis=1, keepdims=True)
-                col = jnp.sum(jnp.where(hot, block_x, 0.0), axis=1, keepdims=True)
-                weight = jnp.where(ids > k, col * (1.0 / pivot), 0.0)
-                xm[j, at] = block_x - weight * (row + jnp.where(hot, 1.0, 0.0))
-
-    piece = rk // 8
-    for b in range(3):
-        eliminate(b * piece, (b + 1) * piece)
+                ahead = jnp.where(near >= 8, slabs[j] / pivots[j], 0.0)
+                unit = jnp.where(near == sub8, 1.0, jnp.where((near >= 0) & (near > sub8) & (near < 8), 0.0, slabs[j]))
+                near_all = col_id - base
+                clear = (row_id - base >= 8) & (near_all >= 0) & (near_all < 8)
+                xm[j] = jnp.where(clear, 0.0, xm[j]) - mm_f32(ahead, unit, TN)
+                xm[j, at] = slabs[j]
+
+    blocks = rk // 8
+    eliminate(0, blocks // 2)
     for j in range(n_out):
         scatter_second(1, j, cbuf, csbuf, cr1, cs2f, cs2b, cr2)
-    for b in range(3, 8):
-        eliminate(b * piece, (b + 1) * piece)
+    eliminate(blocks // 2, blocks)
 
     for j in range(n_out):
         work = xm[j]
@@ -305,6 +328,7 @@
         + [
             pltpu.VMEM((n_out, rk, rk), F32),
             pltpu.VMEM((n_out, 1, rk), F32),
+            pltpu.VMEM((n_out, slots, 2 * rk, rk), BF16),
             pltpu.SemaphoreType.DMA((n_out + 1, 3)),
             pltpu.SemaphoreType.DMA((2, 2 * nx)),
             pltpu.SemaphoreType.DMA((2, 2 * nx)),

time: 123 us -> 72.8 us (0.59)
  Pallas kernels: 119 us -> 68.8 us
    pallas_call x1, Pallas kernels: 119 us -> 68.8 us  [body(): pl.pallas_call(functools.partial(kernel, n_in, n_co), out_shape=(out, out...]
where the time goes in v2:
time: 72.8 us; the launch traced here: 72.6 us
  Pallas kernels  68.8 us (95%)
  local copies, waits for them, and re-layouts  3.14 us (4%)
    pallas_call x1, Pallas kernels, body(): pl.pallas_call(functools.partial(kernel, n_in, n_co), out_shape=(out, out...  68.8 us
    unnamed x2, local copies, waits for them, and re-layouts  3.14 us

profile of v2, /device:TPU:0, one launch (start us, length us, event | category | flops | bytes accessed | tf_op | source)
XLA Modules:
  0.0 72.6 jit_solution(13227631234214824276)
XLA Ops:
  0.6 68.8 %shard_map.86 = (f32[4,64,128]{2,1,0:T(8,128)}, f32[4,64,128]{2,1,0:T(8,128)}) custom-call(bf16[2,512,128]{2,1,0:T(8,128)(2,1)} %left_u.1, bf16[2,512,128]{2,1,0:T(8,128)(2,1)} %left_v.1, bf16[4,8,512,128]{3,2,1,0:T(8,128)(2,1)} %right_u.1, bf16[4,8,512,128]{3,2,1,0:T(8,128)(2,1)} %right_v.1, bf16[4,512,128]{2,1,0:T(8,128)(2,1)} %sketch.1, s32[4,8]{1,0:T(4,128)} %index.1, ...), custom_call_target="tpu_custom_call" | custom-call | tf_op jit(solution)/shard_map/pallas_call | solution.py:309
  69.5 1.6 %copy.11 = f32[4,64,128]{2,1,0:T(8,128)} copy(f32[4,64,128]{2,1,0:T(8,128)} %get-tuple-element.4) | data formatting | bytes 262144
  71.0 1.6 %copy.12 = f32[4,64,128]{2,1,0:T(8,128)} copy(f32[4,64,128]{2,1,0:T(8,128)} %get-tuple-element.5) | data formatting | bytes 262144

commit v3 on v1

--- a/solution.py
+++ b/solution.py
@@ -31,8 +31,8 @@
 
 def kernel(
     n_in, n_co, left_u, left_v, right_u, right_v, sketch, index, mask, basis, coeff,
-    ug, vg, vt, ru, rv, sk, phi, plo, mix, ybuf, sbuf, r1, s2f, s2b, r2, yrow, yb,
-    cbuf, csbuf, cr1, cs2f, cs2b, cr2, crow, xm, scale,
+    ug, vg, vt, ru, rv, sk, pair, probe, mix, ybuf, sbuf, r1, s2f, s2b, r2, yrow, yb,
+    cbuf, csbuf, cr1, cs2f, cs2b, cr2, crow, xm, scale, bt,
     load_sem, gs_sem, gr_sem, rs_send, rs_recv, ag_send, ag_recv,
 ):
     nx = n_co // 2
@@ -111,34 +111,44 @@
             part = block(dst, lax.rem(x + nx - dx, nx) * 2 + (1 - core))
             remote(part, part, gs_sem.at[num, nx + dx], gr_sem.at[num, nx + dx], cols=partner).wait_recv()
 
-    for c in loads:
-        c.wait()
+    for j in range(n_out):
+        loads[3 * j].wait()
+        loads[3 * j + 1].wait()
+        om = jnp.transpose(sk[j])
+
+        @pl.loop(0, slots // 4)
+        def _(quad, j=j, om=om):
+            for s in [quad * 4 + i for i in range(4)]:
+                probe_hi, probe_lo = split(mm(om, rv[j, s], NN))
+                probe[j, s, :rk] = probe_hi
+                probe[j, s, rk:] = probe_lo
+
     forward(0, vg)
     gathered(0, vg)
     own_v.wait()
-    own_u.wait()
 
     @pl.loop(0, tiles)
     def _(t):
         vt[t] = jnp.transpose(vg[t])
 
     for j in range(n_out):
-        om = jnp.transpose(sk[j])
-
-        @pl.loop(0, slots)
-        def _(s, j=j, om=om):
-            k = lax.rem(index[j, s], tiles)
-            live = mask[j, s].astype(F32)
-            probe_hi, probe_lo = split(mm(om, rv[j, s], NN))
-            pair_hi, pair_lo = split(mm(vt[k], ru[j, s], NN))
-            phi[j, s] = pair_hi
-            plo[j, s] = pair_lo
-            mixed = mm(pair_hi, probe_hi, NT) + mm(pair_hi, probe_lo, NT) + mm(pair_lo, probe_hi, NT)
-            mix[j, s] = (mixed * live).astype(BF16)
-
-        if j == 0:
+        loads[3 * j + 2].wait()
+
+        @pl.loop(0, slots // 4)
+        def _(quad, j=j):
+            for s in [quad * 4 + i for i in range(4)]:
+                live = mask[j, s].astype(F32)
+                pair_hi, pair_lo = split(mm(vt[lax.rem(index[j, s], tiles)], ru[j, s], NN))
+                pair[j, s, :, :rk] = pair_hi
+                pair[j, s, :, rk:] = pair_lo
+                wide = mm(pair_hi, probe[j, s], NT)
+                mixed = wide[:, :rk] + wide[:, rk:] + mm(pair_lo, probe[j, s, :rk], NT)
+                mix[j, s] = (mixed * live).astype(BF16)
+
+        if j == n_out // 2:
             forward(1, ug)
 
+    own_u.wait()
     gathered(1, ug)
 
     def scatter_first(phase, j, total, buf, sb, first):
@@ -174,15 +184,7 @@
             total = total + second[j, dz].astype(F32)
         return total
 
-    for j in range(n_out):
-        total = mm(ug[lax.rem(index[j, 0], tiles)], mix[j, 0], NN)
-        for s in range(1, slots):
-            total = total + mm(ug[lax.rem(index[j, s], tiles)], mix[j, s], NN)
-        scatter_first(0, j, total, ybuf, sbuf, r1)
-    for j in range(n_out):
-        scatter_second(0, j, ybuf, sbuf, r1, s2f, s2b, r2)
-
-    for j in range(n_out):
+    def share(j):
         total = scatter_last(0, j, s2f, r2)
         yrow[j] = total
         yb[j, me_in] = total.astype(BF16)
@@ -191,35 +193,41 @@
             go(remote(part, part, ag_send.at[j, 0, dz], ag_recv.at[j, 0, dz], inner=z_at(dz)))
         for dy in range(1, ny):
             go(remote(part, part, ag_send.at[j, dy, 0], ag_recv.at[j, dy, 0], inner=y_at(dy)))
-    for j in range(n_out):
+
+    def relay(j):
         for dz in range(1, nz):
             part = yb.at[j, z_at(nz - dz)]
             remote(part, part, ag_send.at[j, 0, dz], ag_recv.at[j, 0, dz], inner=z_at(dz)).wait_recv()
             for dy in range(1, ny):
                 go(remote(part, part, ag_send.at[j, dy, dz], ag_recv.at[j, dy, dz], inner=y_at(dy)))
 
-    for j in range(n_out):
+    def shared(j):
         for dy in range(1, ny):
             for dz in range(nz):
                 pos = lax.rem(z + nz - dz, nz) * ny + lax.rem(y + ny - dy, ny)
                 part = yb.at[j, pos]
                 remote(part, part, ag_send.at[j, dy, dz], ag_recv.at[j, dy, dz], inner=y_at(dy)).wait_recv()
-        summed_t = jnp.transpose(yb[j].reshape(nb, rk))
-
-        def step(s, total, j=j, summed_t=summed_t):
-            live = mask[j, s].astype(F32)
-            z_hi, z_lo = split(mm(summed_t, ug[lax.rem(index[j, s], tiles)], NN))
-            back = mm(z_hi, phi[j, s], NN) + mm(z_hi, plo[j, s], NN) + mm(z_lo, phi[j, s], NN)
-            b_hi, b_lo = split(back * live)
-            return total + (mm(rv[j, s], b_hi, NT) + mm(rv[j, s], b_lo, NT))
-
-        total = lax.fori_loop(0, slots, step, jnp.zeros((nb, rk), F32))
-        scatter_first(1, j, total, cbuf, csbuf, cr1)
+
+    for j in range(n_out):
+        total = mm(ug[lax.rem(index[j, 0], tiles)], mix[j, 0], NN)
+        for s in range(1, slots):
+            total = total + mm(ug[lax.rem(index[j, s], tiles)], mix[j, s], NN)
+        scatter_first(0, j, total, ybuf, sbuf, r1)
+        if j >= 1:
+            scatter_second(0, j - 1, ybuf, sbuf, r1, s2f, s2b, r2)
+    scatter_second(0, n_out - 1, ybuf, sbuf, r1, s2f, s2b, r2)
+    for j in range(n_out):
+        share(j)
+        if j >= 1:
+            relay(j - 1)
+    relay(n_out - 1)
 
     row_id = lax.broadcasted_iota(jnp.int32, (rk, rk), 0)
     col_id = lax.broadcasted_iota(jnp.int32, (rk, rk), 1)
-    lane = lax.broadcasted_iota(jnp.int32, (1, rk), 1)
-    for j in range(n_out):
+    sub8 = lax.broadcasted_iota(jnp.int32, (8, rk), 0)
+    lane8 = lax.broadcasted_iota(jnp.int32, (8, rk), 1)
+
+    def normal(j):
         summed = yb[j].reshape(nb, rk)
         gram = mm(summed, summed, TN)
         diag = jnp.where(row_id == col_id, gram, 0.0)
@@ -228,28 +236,75 @@
         scale[j] = s_row
         xm[j] = gram * s_col * s_row
 
-    def eliminate(start, stop):
-        ids = lax.broadcasted_iota(jnp.int32, (rk - start, 1), 0) + start
-        at = pl.ds(start, rk - start)
-
-        @pl.loop(start, stop)
-        def _(k):
-            hot = lane == k
+    def eliminate(b):
+        base = pl.multiple_of(b * 8, 8)
+        near = lane8 - base
+        at = pl.ds(base, 8)
+        slabs = [xm[j, at] for j in range(n_out)]
+        cols = [
+            [
+                jnp.broadcast_to(jnp.sum(jnp.where(near == i, slab, 0.0), axis=1, keepdims=True), (8, rk))
+                for i in range(8)
+            ]
+            for slab in slabs
+        ]
+        pivots = [jnp.ones((8, rk), F32)] * n_out
+        for k in range(8):
+            hot = jnp.where(near[:1] == k, 1.0, 0.0)
             for j in range(n_out):
-                block_x = xm[j, at]
-                row = xm[j, pl.ds(k, 1)]
-                pivot = jnp.sum(jnp.where(hot, row, 0.0), axis=1, keepdims=True)
-                col = jnp.sum(jnp.where(hot, block_x, 0.0), axis=1, keepdims=True)
-                weight = jnp.where(ids > k, col * (1.0 / pivot), 0.0)
-                xm[j, at] = block_x - weight * (row + jnp.where(hot, 1.0, 0.0))
-
-    piece = rk // 8
-    for b in range(3):
-        eliminate(b * piece, (b + 1) * piece)
-    for j in range(n_out):
-        scatter_second(1, j, cbuf, csbuf, cr1, cs2f, cs2b, cr2)
-    for b in range(3, 8):
-        eliminate(b * piece, (b + 1) * piece)
+                column = cols[j][k]
+                pivots[j] = jnp.where(sub8 == k, column[k : k + 1], pivots[j])
+                weight = jnp.where(sub8 > k, column * (1.0 / column[k : k + 1]), 0.0)
+                slabs[j] = slabs[j] - weight * (slabs[j][k : k + 1] + hot)
+                for i in range(k + 1, 8):
+                    cols[j][i] = cols[j][i] - weight * cols[j][i][k : k + 1]
+        for j in range(n_out):
+            ahead = jnp.where(near >= 8, slabs[j] / pivots[j], 0.0)
+            unit = jnp.where(near == sub8, 1.0, jnp.where((near >= 0) & (near > sub8) & (near < 8), 0.0, slabs[j]))
+            near_all = col_id - base
+            clear = (row_id - base >= 8) & (near_all >= 0) & (near_all < 8)
+            xm[j] = jnp.where(clear, 0.0, xm[j]) - mm_f32(ahead, unit, TN)
+            xm[j, at] = slabs[j]
+
+    blocks = rk // 8
+
+    def back_slot(j, s, summed_t):
+        live = mask[j, s].astype(F32)
+        z_hi, z_lo = split(mm(summed_t, ug[lax.rem(index[j, s], tiles)], NN))
+        wide = mm(z_hi, pair[j, s], NN)
+        back = wide[:, :rk] + wide[:, rk:] + mm(z_lo, pair[j, s, :, :rk], NN)
+        b_hi, b_lo = split(back * live)
+        bt[j, s, :rk] = b_hi
+        bt[j, s, rk:] = b_lo
+
+    for j in range(n_out):
+        shared(j)
+        summed_t = jnp.transpose(yb[j].reshape(nb, rk))
+
+        @pl.loop(0, slots // 4)
+        def _(quad, j=j, summed_t=summed_t):
+            for i in range(4):
+                back_slot(j, quad * 4 + i, summed_t)
+
+        wide = mm(rv[j, 0], bt[j, 0], NT)
+        for s in range(1, slots):
+            wide = wide + mm(rv[j, s], bt[j, s], NT)
+        scatter_first(1, j, wide[:, :rk] + wide[:, rk:], cbuf, csbuf, cr1)
+        if j >= 1:
+            scatter_second(1, j - 1, cbuf, csbuf, cr1, cs2f, cs2b, cr2)
+
+    for j in range(n_out):
+        normal(j)
+
+    @pl.loop(0, blocks // 4)
+    def _(b):
+        eliminate(b)
+
+    scatter_second(1, n_out - 1, cbuf, csbuf, cr1, cs2f, cs2b, cr2)
+
+    @pl.loop(blocks // 4, blocks)
+    def _(b):
+        eliminate(b)
 
     for j in range(n_out):
         work = xm[j]
@@ -295,8 +350,8 @@
             pltpu.VMEM((n_out, slots, nb, rk), BF16),
             pltpu.VMEM((n_out, slots, nb, rk), BF16),
             pltpu.VMEM((n_out, nb, rk), BF16),
-            pltpu.VMEM((n_out, slots, rk, rk), BF16),
-            pltpu.VMEM((n_out, slots, rk, rk), BF16),
+            pltpu.VMEM((n_out, slots, rk, 2 * rk), BF16),
+            pltpu.VMEM((n_out, slots, 2 * rk, rk), BF16),
             pltpu.VMEM((n_out, slots, rk, rk), BF16),
         ]
         + wire
@@ -305,6 +360,7 @@
         + [
             pltpu.VMEM((n_out, rk, rk), F32),
             pltpu.VMEM((n_out, 1, rk), F32),
+            pltpu.VMEM((n_out, slots, 2 * rk, rk), BF16),
             pltpu.SemaphoreType.DMA((n_out + 1, 3)),
             pltpu.SemaphoreType.DMA((2, 2 * nx)),
             pltpu.SemaphoreType.DMA((2, 2 * nx)),

time: 123 us -> 74.7 us (0.61)
  Pallas kernels: 119 us -> 70.7 us
    pallas_call x1, Pallas kernels: 119 us -> 70.7 us  [body(): pl.pallas_call(functools.partial(kernel, n_in, n_co), out_shape=(out, out...]
where the time goes in v3:
time: 74.7 us; the launch traced here: 74.5 us
  Pallas kernels  70.7 us (95%)
  local copies, waits for them, and re-layouts  3.14 us (4%)
    pallas_call x1, Pallas kernels, body(): pl.pallas_call(functools.partial(kernel, n_in, n_co), out_shape=(out, out...  70.7 us
    unnamed x2, local copies, waits for them, and re-layouts  3.14 us

profile of v3, /device:TPU:0, one launch (start us, length us, event | category | flops | bytes accessed | tf_op | source)
XLA Modules:
  0.0 74.5 jit_solution(3878162265717997621)
XLA Ops:
  0.6 70.7 %shard_map.86 = (f32[4,64,128]{2,1,0:T(8,128)}, f32[4,64,128]{2,1,0:T(8,128)}) custom-call(bf16[2,512,128]{2,1,0:T(8,128)(2,1)} %left_u.1, bf16[2,512,128]{2,1,0:T(8,128)(2,1)} %left_v.1, bf16[4,8,512,128]{3,2,1,0:T(8,128)(2,1)} %right_u.1, bf16[4,8,512,128]{3,2,1,0:T(8,128)(2,1)} %right_v.1, bf16[4,512,128]{2,1,0:T(8,128)(2,1)} %sketch.1, s32[4,8]{1,0:T(4,128)} %index.1, ...), custom_call_target="tpu_custom_call" | custom-call | tf_op jit(solution)/shard_map/pallas_call | solution.py:341
  71.3 1.6 %copy.11 = f32[4,64,128]{2,1,0:T(8,128)} copy(f32[4,64,128]{2,1,0:T(8,128)} %get-tuple-element.4) | data formatting | bytes 262144
  72.9 1.6 %copy.12 = f32[4,64,128]{2,1,0:T(8,128)} copy(f32[4,64,128]{2,1,0:T(8,128)} %get-tuple-element.5) | data formatting | bytes 262144
